TPU v7x, 512 devices: a whole 4x4x16 slice. The times are simulated.
512 devices in a mesh: sec: 2 (over z_hi), gx: 16 (over z_lo, core), gy: 16 (over x, y).
Axes of the slice: x: 4, y: 4, z: 16 (z_hi: 2, z_lo: 8; z = z_hi * 8 + z_lo), core: 2. Of those that a mesh axis runs over, the one named last changes fastest.
Arguments:
- terminal: float32 [4, 16, 256, 4096], P('sec', None, 'gx', 'gy'), may hold values from -6 to 6
- forward_temp: bfloat16 [2, 4, 16, 256, 4096], P(None, 'sec', None, 'gx', 'gy'), may hold values from -6 to 6
- conductivity: float32 [16, 256, 4096], P(None, 'gx', 'gy'), may hold values from 0.02 to 0.15
- velocity: float32 [2, 16, 256, 4096], P(None, None, 'gx', 'gy'), may hold values from -0.3 to 0.3
- fixed_mask: int32 [16, 256, 4096], P(None, 'gx', 'gy'), may hold values 0 or 1
- wells: int32 [4, 8, 3], P('sec'), may hold values from 0 to 4095, as said below
- misfit: float32 [2, 4, 8], P(None, 'sec'), may hold values from -12 to 12
- head_gradient: bfloat16 [2, 16, 256, 4096], P('sec', None, 'gx', 'gy'), may hold values from -6 to 6
- blocks: bfloat16 [32, 7, 128, 128], P('gy'), may hold values from -0.1875 to 0.1875
- block_cols: int32 [32, 7], P('gy'), may hold values from 0 to 31, as said below
Outputs:
- head_adjoint: float32 [2, 16, 256, 4096], P('sec', None, 'gx', 'gy')
- sensitivity: float32 [16, 256, 4096], P(None, 'gx', 'gy')
Inputs may be any that keep to these rules, and one draw needn't show every extreme that they name: `wells`: each row is one cell (z, x, y) with z < 16, x < 256, y < 4096; the first test observes the cells (0, 0, 0) and (15, 255, 4095). `block_cols`: row r lists 7 different block columns, the first of which is r.
All inputs are finite; a program needn't handle non-finite values. No bound on the sum of `fixed_mask` on one device may be relied on, other than what follows from the above.
Results may differ from a plain program's by a relative error of at most 0.0029.
Values may be sent and summed in bfloat16 or wider, within the bound.
No kernel may reach another device: no remote copies, remote signals or barrier semaphores. Data moves between devices by JAX's collectives and lax.ppermute only.
A program may use at most 64 MiB of HBM per device.

v0:
```python
import jax
import jax.numpy as jnp
from jax import lax
from jax.sharding import PartitionSpec as P


def extended(cells, sides, width):
    for axis, dim in sides:
        count = lax.axis_size(axis)
        ends = count - 1
        head = lax.slice_in_dim(cells, 0, width, axis=dim)
        tail = lax.slice_in_dim(cells, cells.shape[dim] - width, cells.shape[dim], axis=dim)
        cells = jnp.concatenate(
            [
                lax.ppermute(tail, axis, [(i, (i + 1) % count) for i in range(ends)]),
                cells,
                lax.ppermute(head, axis, [((i + 1) % count, i) for i in range(ends)]),
            ],
            axis=dim,
        )
    return cells


def shifted(padded):
    lead = [(0, 0)] * (padded.ndim - 3)
    deeper = jnp.pad(padded, lead + [(1, 1), (0, 0), (0, 0)])
    centre = deeper[..., 1:-1, 1:-1, 1:-1]
    beside_all = [
        deeper[..., 2:, 1:-1, 1:-1],
        deeper[..., :-2, 1:-1, 1:-1],
        deeper[..., 1:-1, 2:, 1:-1],
        deeper[..., 1:-1, :-2, 1:-1],
        deeper[..., 1:-1, 1:-1, 2:],
        deeper[..., 1:-1, 1:-1, :-2],
    ]
    return (centre, beside_all)


def face_weights(kappa_pad):
    centre, beside_all = shifted(kappa_pad)
    return [
        2.0 * centre * other / jnp.where(centre + other > 0.0, centre + other, 1.0)
        for other in beside_all
    ]


def advance(adjoint_pad, weights, keep, speed_x, speed_y, source):
    centre, beside_all = shifted(adjoint_pad)
    diffusion = weights[0] * (beside_all[0] - centre)
    for face in range(1, 6):
        diffusion = diffusion + weights[face] * (beside_all[face] - centre)
    slope_x = 0.5 * (beside_all[2] - beside_all[3])
    slope_y = 0.5 * (beside_all[4] - beside_all[5])
    updated = keep * (centre + diffusion + speed_x * slope_x + speed_y * slope_y + source)
    return (updated, diffusion, slope_x, slope_y)


def well_sources(wells, misfit_level, layers, rows_x, cols_y, margin):
    start_x = lax.axis_index("gx") * rows_x - margin
    start_y = lax.axis_index("gy") * cols_y - margin
    coord_z = jnp.arange(layers, dtype=jnp.int32)[:, None, None]
    coord_x = (start_x + jnp.arange(rows_x + 2 * margin, dtype=jnp.int32))[None, :, None]
    coord_y = (start_y + jnp.arange(cols_y + 2 * margin, dtype=jnp.int32))[None, None, :]
    well_z = wells[:, :, 0][:, :, None, None, None]
    well_x = wells[:, :, 1][:, :, None, None, None]
    well_y = wells[:, :, 2][:, :, None, None, None]
    matches = (coord_z == well_z) & (coord_x == well_x) & (coord_y == well_y)
    return jnp.sum(jnp.where(matches, misfit_level[:, :, None, None, None], 0.0), axis=1)


def shards(
    terminal,
    forward_temp,
    conductivity,
    velocity,
    fixed_mask,
    wells,
    misfit,
    head_gradient,
    blocks,
    block_cols,
):
    layers, rows_x, cols_y = conductivity.shape
    steps = forward_temp.shape[0]
    keep = 1.0 - fixed_mask.astype(jnp.float32)
    heat_sens = jnp.zeros((layers, rows_x, cols_y), jnp.float32)
    flow_x = jnp.zeros((layers, rows_x, cols_y), jnp.float32)
    flow_y = jnp.zeros((layers, rows_x, cols_y), jnp.float32)
    kappa_pad = extended(conductivity, (("gx", 1), ("gy", 2)), 1)
    weights = face_weights(kappa_pad)
    adjoint = terminal
    for level in reversed(range(steps)):
        padded = extended(adjoint, (("gx", 2), ("gy", 3)), 1)
        source = well_sources(wells, misfit[level], layers, rows_x, cols_y, 0)
        adjoint, diffusion, slope_x, slope_y = advance(
            padded, weights, keep, velocity[0], velocity[1], source
        )
        temper = forward_temp[level].astype(jnp.float32)
        heat_sens = heat_sens + jnp.sum(temper * diffusion, axis=0)
        flow_x = flow_x + jnp.sum(temper * slope_x, axis=0)
        flow_y = flow_y + jnp.sum(temper * slope_y, axis=0)
    summed = lax.psum_scatter(jnp.stack([flow_x, flow_y]), "sec", scatter_dimension=0, tiled=True)
    rounded = summed[0].astype(jnp.bfloat16)
    row_blocks, per_row, block_size, _ = blocks.shape
    piece = lax.all_gather(rounded, "gy", axis=2, tiled=True)
    count = piece.shape[2] // block_size
    split_rows = piece.reshape(layers, rows_x, count, block_size)
    block_ids = jnp.arange(count, dtype=jnp.int32)
    chosen = (block_cols[:, :, None] == block_ids[None, None, :]).astype(jnp.bfloat16)
    portion = jnp.einsum("bkq,zxqj->bkzxj", chosen, split_rows, preferred_element_type=jnp.float32)
    picked = portion.astype(jnp.bfloat16)
    head = jnp.einsum(
        "bkzxj,bkij->zxbi", picked, blocks, preferred_element_type=jnp.float32
    ).reshape(layers, rows_x, cols_y)
    partial_sens = heat_sens + head * head_gradient[0].astype(jnp.float32)
    sensitivity = lax.psum(partial_sens, "sec")
    return (head[None], sensitivity)


def solution(mesh):
    placed = (
        P("sec", None, "gx", "gy"),
        P(None, "sec", None, "gx", "gy"),
        P(None, "gx", "gy"),
        P(None, None, "gx", "gy"),
        P(None, "gx", "gy"),
        P("sec", None, None),
        P(None, "sec", None),
        P("sec", None, "gx", "gy"),
        P("gy", None, None, None),
        P("gy", None),
    )
    return jax.shard_map(
        shards,
        mesh=mesh,
        in_specs=placed,
        out_specs=(P("sec", None, "gx", "gy"), P(None, "gx", "gy")),
        check_vma=False,
    )
```

profile of v0, /device:TPU:1, one launch (start us, length us, event | category | flops | bytes accessed | tf_op | source)
XLA Modules:
  0.0 278.9 jit_solution(739867863807899032)
XLA Ops:
  7.3 1.1 fusion.57
  8.3 4.9 %collective-permute-start.2 = (f32[16,1,256]{2,1,0:T(1,128)S(1)}, f32[16,1,256]{2,1,0:T(1,128)S(1)}, u32[]{:S(2)}, u32[]{:S(2)}) collective-permute-start(f32[16,1,256]{2,1,0:T(1,128)S(1)} %get-tuple-element.29), channel_id=1, source_target_pairs={{0,16},{16,32},{32,48},{48,64},{64,80},{80,96},{96,112},{112,128},... | collective-permute-start | bytes 49160 | tf_op jit(solution)/shard_map/ppermute | solution.py:15
  13.3 5.1 %collective-permute-start.3 = (f32[16,1,256]{2,1,0:T(1,128)S(1)}, f32[16,1,256]{2,1,0:T(1,128)S(1)}, u32[]{:S(2)}, u32[]{:S(2)}) collective-permute-start(f32[16,1,256]{2,1,0:T(1,128)S(1)} %get-tuple-element.30), channel_id=1, source_target_pairs={{16,0},{32,16},{48,32},{64,48},{80,64},{96,80},{112,96},{128,112},... | collective-permute-start | bytes 49160 | tf_op jit(solution)/shard_map/ppermute | solution.py:17
  18.4 1.1 fusion.55
  19.5 1.9 collective-permute-start
  21.4 3.6 %collective-permute-start.1 = (f32[2,16,1,256]{3,2,1,0:T(1,128)S(1)}, f32[2,16,1,256]{3,2,1,0:T(1,128)S(1)}, u32[]{:S(2)}, u32[]{:S(2)}) collective-permute-start(f32[2,16,1,256]{3,2,1,0:T(1,128)S(1)} %get-tuple-element.20), channel_id=1, source_target_pairs={{0,16},{16,32},{32,48},{48,64},{64,80},{80,96},{96,112},{112,128},... | collective-permute-start | bytes 98312 | tf_op jit(solution)/shard_map/ppermute | solution.py:15
  25.9 1.1 multiply_bitcast_fusion.1
  27.5 1.4 collective-permute-start.4
  28.9 1.3 collective-permute-start.5
  31.1 1.5 collective-permute-done.4
  32.6 4.1 %collective-permute-done.5 = f32[16,18,1]{2,1,0:T(8,128)S(1)} collective-permute-done((f32[16,18,1]{2,1,0:T(8,128)S(1)}, f32[16,18,1]{2,1,0:T(8,128)S(1)}, u32[]{:S(2)}, u32[]{:S(2)}) %collective-permute-start.5) | collective-permute-done | bytes 1184 | tf_op jit(solution)/shard_map/ppermute | solution.py:17
  37.4 2.2 collective-permute-start.6
  39.6 1.3 collective-permute-start.7
  41.5 6.3 %collective-permute-done.6 = f32[2,16,18,1]{3,2,1,0:T(8,128)S(1)} collective-permute-done((f32[2,16,18,1]{3,2,1,0:T(8,128)S(1)}, f32[2,16,18,1]{3,2,1,0:T(8,128)S(1)}, u32[]{:S(2)}, u32[]{:S(2)}) %collective-permute-start.6) | collective-permute-done | bytes 2336 | tf_op jit(solution)/shard_map/ppermute | solution.py:15
  47.8 3.8 %collective-permute-done.7 = f32[2,16,18,1]{3,2,1,0:T(8,128)S(1)} collective-permute-done((f32[2,16,18,1]{3,2,1,0:T(8,128)S(1)}, f32[2,16,18,1]{3,2,1,0:T(8,128)S(1)}, u32[]{:S(2)}, u32[]{:S(2)}) %collective-permute-start.7) | collective-permute-done | bytes 2336 | tf_op jit(solution)/shard_map/ppermute | solution.py:17
  52.3 1.1 add_multiply_fusion
  53.5 3.3 %collective-permute-start.8 = (f32[2,16,1,256]{3,2,1,0:T(1,128)S(1)}, f32[2,16,1,256]{3,2,1,0:T(1,128)S(1)}, u32[]{:S(2)}, u32[]{:S(2)}) collective-permute-start(f32[2,16,1,256]{3,2,1,0:T(1,128)S(1)} %get-tuple-element.15), channel_id=1, source_target_pairs={{16,0},{32,16},{48,32},{64,48},{80,64},{96,80},{112,96},{128,112},... | collective-permute-start | bytes 98312 | tf_op jit(solution)/shard_map/ppermute | solution.py:17
  56.8 3.8 %collective-permute-start.9 = (f32[2,16,1,256]{3,2,1,0:T(1,128)S(1)}, f32[2,16,1,256]{3,2,1,0:T(1,128)S(1)}, u32[]{:S(2)}, u32[]{:S(2)}) collective-permute-start(f32[2,16,1,256]{3,2,1,0:T(1,128)S(1)} %get-tuple-element.16), channel_id=1, source_target_pairs={{0,16},{16,32},{32,48},{48,64},{64,80},{80,96},{96,112},{112,128},... | collective-permute-start | bytes 98312 | tf_op jit(solution)/shard_map/ppermute | solution.py:15
  60.6 1.0 collective-permute-done.9
  61.9 1.3 collective-permute-start.10
  63.2 5.1 %collective-permute-start.11 = (f32[2,16,18,1]{3,2,1,0:T(8,128)S(1)}, f32[2,16,18,1]{3,2,1,0:T(8,128)S(1)}, u32[]{:S(2)}, u32[]{:S(2)}) collective-permute-start(f32[2,16,18,1]{3,2,1,0:T(8,128)S(1)} %get-tuple-element.12), channel_id=1, source_target_pairs={{0,1},{1,2},{2,3},{3,4},{4,5},{5,6},{6,7},{7,8},{8,9},{9,10},{10,1... | collective-permute-start | bytes 6920 | tf_op jit(solution)/shard_map/ppermute | solution.py:15
  68.9 5.6 %collective-permute-done.10 = f32[2,16,18,1]{3,2,1,0:T(8,128)S(1)} collective-permute-done((f32[2,16,18,1]{3,2,1,0:T(8,128)S(1)}, f32[2,16,18,1]{3,2,1,0:T(8,128)S(1)}, u32[]{:S(2)}, u32[]{:S(2)}) %collective-permute-start.10) | collective-permute-done | bytes 2336 | tf_op jit(solution)/shard_map/ppermute | solution.py:17
  74.5 1.8 collective-permute-done.11
  76.2 1.3 fusion.7
  78.5 59.7 %reduce-scatter.2.cloned.1.call-done = f32[1,16,16,256]{3,2,1,0:T(8,128)} async-done(((f32[2,16,16,256]{3,2,1,0:T(8,128)}), f32[1,16,16,256]{3,2,1,0:T(8,128)}) %reduce-scatter.2.cloned.1.call-update) | async-done | bytes 262160 | tf_op jit(solution)/shard_map/reduce_scatter | solution.py:102
  138.3 1.6 convert_element_type.41
  141.0 1.7 fusion.9
  142.7 52.4 %all-gather.3.cloned.1.call-done = bf16[1,16,16,4096]{3,2,1,0:T(8,128)(2,1)} async-done(((bf16[1,16,16,256]{3,2,1,0:T(8,128)(2,1)}), bf16[1,16,16,4096]{3,2,1,0:T(8,128)(2,1)}) %all-gather.3.cloned.1.call-update) | async-done | bytes 2097168 | tf_op jit(solution)/shard_map/all_gather | solution.py:105
  195.1 2.1 copy.21
  199.8 0.9 broadcast_in_dim_reshape.3
  200.7 70.0 %all-reduce.5.cloned.1.call-done = f32[16,16,256]{2,1,0:T(8,128)} async-done(((f32[16,16,256]{2,1,0:T(8,128)}), f32[16,16,256]{2,1,0:T(8,128)}) %all-reduce.5.cloned.1.call-update) | async-done | bytes 262160 | tf_op jit(solution)/shard_map/psum | solution.py:116
  270.7 1.7 copy.26
  (61 shorter events, 9.7 us)
Async XLA Ops:
  7.2 190.6 %copy-start = (bf16[2,7,128,128]{3,2,1,0:T(8,128)(2,1)S(1)}, bf16[2,7,128,128]{3,2,1,0:T(8,128)(2,1)}, u32[]{:S(2)}) copy-start(bf16[2,7,128,128]{3,2,1,0:T(8,128)(2,1)} %param.18) | copy-start | bytes 1376260
  7.2 20.1 %copy-start.2 = (f32[16,16,256]{2,1,0:T(8,128)S(1)}, f32[16,16,256]{2,1,0:T(8,128)}, u32[]{:S(2)}) copy-start(f32[16,16,256]{2,1,0:T(8,128)} %param.12) | copy-start | bytes 786436
  7.2 19.8 %copy-start.7 = (s32[16,16,256]{2,1,0:T(8,128)S(1)}, s32[16,16,256]{2,1,0:T(8,128)}, u32[]{:S(2)}) copy-start(s32[16,16,256]{2,1,0:T(8,128)} %param.14) | copy-start | bytes 786436
  7.2 20.1 %copy-start.10 = (f32[2,2,8]{2,1,0:T(2,128)S(1)}, f32[2,2,8]{2,1,0:T(2,128)}, u32[]{:S(2)}) copy-start(f32[2,2,8]{2,1,0:T(2,128)} %param.16) | copy-start | bytes 388
  7.2 131.1 %reduce-scatter.2.cloned.1.call-start = ((), (), s32[]{:S(2)}) async-start(), calls=%async_computation.1 | async-start | bytes 786432 | tf_op jit(solution)/shard_map/reduce_scatter | solution.py:102
  8.3 18.9 %collective-permute-start.2 = (f32[16,1,256]{2,1,0:T(1,128)S(1)}, f32[16,1,256]{2,1,0:T(1,128)S(1)}, u32[]{:S(2)}, u32[]{:S(2)}) collective-permute-start(f32[16,1,256]{2,1,0:T(1,128)S(1)} %get-tuple-element.29), channel_id=1, source_target_pairs={{0,16},{16,32},{32,48},{48,64},{64,80},{80,96},{96,112},{112,128},... | collective-permute-start | bytes 49160 | tf_op jit(solution)/shard_map/ppermute | solution.py:15
  13.3 14.0 %collective-permute-start.3 = (f32[16,1,256]{2,1,0:T(1,128)S(1)}, f32[16,1,256]{2,1,0:T(1,128)S(1)}, u32[]{:S(2)}, u32[]{:S(2)}) collective-permute-start(f32[16,1,256]{2,1,0:T(1,128)S(1)} %get-tuple-element.30), channel_id=1, source_target_pairs={{16,0},{32,16},{48,32},{64,48},{80,64},{96,80},{112,96},{128,112},... | collective-permute-start | bytes 49160 | tf_op jit(solution)/shard_map/ppermute | solution.py:17
  19.5 17.6 %collective-permute-start = (f32[2,16,1,256]{3,2,1,0:T(1,128)S(1)}, f32[2,16,1,256]{3,2,1,0:T(1,128)S(1)}, u32[]{:S(2)}, u32[]{:S(2)}) collective-permute-start(f32[2,16,1,256]{3,2,1,0:T(1,128)S(1)} %get-tuple-element.19), channel_id=1, source_target_pairs={{16,0},{32,16},{48,32},{64,48},{80,64},{96,80},{112,96},{128,112},... | collective-permute-start | bytes 98312 | tf_op jit(solution)/shard_map/ppermute | solution.py:17
  21.4 15.7 %collective-permute-start.1 = (f32[2,16,1,256]{3,2,1,0:T(1,128)S(1)}, f32[2,16,1,256]{3,2,1,0:T(1,128)S(1)}, u32[]{:S(2)}, u32[]{:S(2)}) collective-permute-start(f32[2,16,1,256]{3,2,1,0:T(1,128)S(1)} %get-tuple-element.20), channel_id=1, source_target_pairs={{0,16},{16,32},{32,48},{48,64},{64,80},{80,96},{96,112},{112,128},... | collective-permute-start | bytes 98312 | tf_op jit(solution)/shard_map/ppermute | solution.py:15
  27.4 9.7 %copy-start.1 = (f32[2,16,16,256]{3,2,1,0:T(8,128)S(1)}, f32[2,16,16,256]{3,2,1,0:T(8,128)}, u32[]{:S(2)}) copy-start(f32[2,16,16,256]{3,2,1,0:T(8,128)} %param.10) | copy-start | bytes 1572868
  27.5 5.1 %collective-permute-start.4 = (f32[16,18,1]{2,1,0:T(8,128)S(1)}, f32[16,18,1]{2,1,0:T(8,128)S(1)}, u32[]{:S(2)}, u32[]{:S(2)}) collective-permute-start(f32[16,18,1]{2,1,0:T(8,128)S(1)} %get-tuple-element.22), channel_id=1, source_target_pairs={{0,1},{1,2},{2,3},{3,4},{4,5},{5,6},{6,7},{7,8},{8,9},{9,10},{10,1... | collective-permute-start | bytes 3464 | tf_op jit(solution)/shard_map/ppermute | solution.py:15
  28.9 7.8 %collective-permute-start.5 = (f32[16,18,1]{2,1,0:T(8,128)S(1)}, f32[16,18,1]{2,1,0:T(8,128)S(1)}, u32[]{:S(2)}, u32[]{:S(2)}) collective-permute-start(f32[16,18,1]{2,1,0:T(8,128)S(1)} %get-tuple-element.21), channel_id=1, source_target_pairs={{1,0},{2,1},{3,2},{4,3},{5,4},{6,5},{7,6},{8,7},{9,8},{10,9},{11,1... | collective-permute-start | bytes 3464 | tf_op jit(solution)/shard_map/ppermute | solution.py:17
  37.4 10.4 %collective-permute-start.6 = (f32[2,16,18,1]{3,2,1,0:T(8,128)S(1)}, f32[2,16,18,1]{3,2,1,0:T(8,128)S(1)}, u32[]{:S(2)}, u32[]{:S(2)}) collective-permute-start(f32[2,16,18,1]{3,2,1,0:T(8,128)S(1)} %get-tuple-element.14), channel_id=1, source_target_pairs={{0,1},{1,2},{2,3},{3,4},{4,5},{5,6},{6,7},{7,8},{8,9},{9,10},{10,1... | collective-permute-start | bytes 6920 | tf_op jit(solution)/shard_map/ppermute | solution.py:15
  39.6 12.0 %collective-permute-start.7 = (f32[2,16,18,1]{3,2,1,0:T(8,128)S(1)}, f32[2,16,18,1]{3,2,1,0:T(8,128)S(1)}, u32[]{:S(2)}, u32[]{:S(2)}) collective-permute-start(f32[2,16,18,1]{3,2,1,0:T(8,128)S(1)} %get-tuple-element.13), channel_id=1, source_target_pairs={{1,0},{2,1},{3,2},{4,3},{5,4},{6,5},{7,6},{8,7},{9,8},{10,9},{11,1... | collective-permute-start | bytes 6920 | tf_op jit(solution)/shard_map/ppermute | solution.py:17
  53.5 7.1 %collective-permute-start.8 = (f32[2,16,1,256]{3,2,1,0:T(1,128)S(1)}, f32[2,16,1,256]{3,2,1,0:T(1,128)S(1)}, u32[]{:S(2)}, u32[]{:S(2)}) collective-permute-start(f32[2,16,1,256]{3,2,1,0:T(1,128)S(1)} %get-tuple-element.15), channel_id=1, source_target_pairs={{16,0},{32,16},{48,32},{64,48},{80,64},{96,80},{112,96},{128,112},... | collective-permute-start | bytes 98312 | tf_op jit(solution)/shard_map/ppermute | solution.py:17
  56.8 11.5 %copy-start.3 = (bf16[2,2,16,16,256]{4,3,2,1,0:T(8,128)(2,1)S(1)}, bf16[2,2,16,16,256]{4,3,2,1,0:T(8,128)(2,1)}, u32[]{:S(2)}) copy-start(bf16[2,2,16,16,256]{4,3,2,1,0:T(8,128)(2,1)} %param.11) | copy-start | bytes 1572868
  56.8 4.8 %collective-permute-start.9 = (f32[2,16,1,256]{3,2,1,0:T(1,128)S(1)}, f32[2,16,1,256]{3,2,1,0:T(1,128)S(1)}, u32[]{:S(2)}, u32[]{:S(2)}) collective-permute-start(f32[2,16,1,256]{3,2,1,0:T(1,128)S(1)} %get-tuple-element.16), channel_id=1, source_target_pairs={{0,16},{16,32},{32,48},{48,64},{64,80},{80,96},{96,112},{112,128},... | collective-permute-start | bytes 98312 | tf_op jit(solution)/shard_map/ppermute | solution.py:15
  61.9 12.6 %collective-permute-start.10 = (f32[2,16,18,1]{3,2,1,0:T(8,128)S(1)}, f32[2,16,18,1]{3,2,1,0:T(8,128)S(1)}, u32[]{:S(2)}, u32[]{:S(2)}) collective-permute-start(f32[2,16,18,1]{3,2,1,0:T(8,128)S(1)} %get-tuple-element.11), channel_id=1, source_target_pairs={{1,0},{2,1},{3,2},{4,3},{5,4},{6,5},{7,6},{8,7},{9,8},{10,9},{11,1... | collective-permute-start | bytes 6920 | tf_op jit(solution)/shard_map/ppermute | solution.py:17
  63.2 13.0 %collective-permute-start.11 = (f32[2,16,18,1]{3,2,1,0:T(8,128)S(1)}, f32[2,16,18,1]{3,2,1,0:T(8,128)S(1)}, u32[]{:S(2)}, u32[]{:S(2)}) collective-permute-start(f32[2,16,18,1]{3,2,1,0:T(8,128)S(1)} %get-tuple-element.12), channel_id=1, source_target_pairs={{0,1},{1,2},{2,3},{3,4},{4,5},{5,6},{6,7},{7,8},{8,9},{9,10},{10,1... | collective-permute-start | bytes 6920 | tf_op jit(solution)/shard_map/ppermute | solution.py:15
  78.5 116.6 %all-gather.3.cloned.1.call-start = ((), (), s32[]{:S(2)}) async-start(), calls=%async_computation.3 | async-start | bytes 2228224 | tf_op jit(solution)/shard_map/all_gather | solution.py:105
  139.9 130.8 %all-reduce.5.cloned.1.call-start = ((), (), s32[]{:S(2)}) async-start(), calls=%async_computation.2 | async-start | bytes 524288 | tf_op jit(solution)/shard_map/psum | solution.py:116
  140.0 1.0 copy-start.4
  195.1 2.1 copy-start.9
  197.7 1.0 copy-start.5
  197.7 1.0 copy-start.6
  197.8 1.0 copy-start.8
Sparse Core Ops, SparseCore 0:
  78.6 59.6 reduce-scatter.1
  141.7 53.3 all-gather.2
  199.7 70.9 all-reduce.4
where the time goes:
time: 280 us; the launch traced here: 279 us
  waiting for transfers between devices  206 us (74%)
  starting transfers between devices  35.4 us (13%)
  between operations  14.1 us (5%)
  other arithmetic  12.9 us (5%)
  local copies, waits for them, and re-layouts  9.19 us (3%)
    psum x1, waiting for transfers between devices, shards(): sensitivity = lax.psum(partial_sens, 'sec')  70 us
    reduce_scatter x1, waiting for transfers between devices, shards(): lax.psum_scatter(jnp.stack([flow_x, flow_y]), 'sec', scatter_dimension=0,...  59.7 us
    all_gather x1, waiting for transfers between devices, shards(): piece = lax.all_gather(rounded, 'gy', axis=2, tiled=True)  52.4 us
    ppermute x6, starting transfers between devices, extended(): lax.ppermute(tail, axis, [(i, (i + 1) % count) for i in range(ends)])  21 us
    ppermute x6, starting transfers between devices, extended(): lax.ppermute(head, axis, [((i + 1) % count, i) for i in range(ends)])  14.3 us
    ppermute x6, waiting for transfers between devices, extended(): lax.ppermute(head, axis, [((i + 1) % count, i) for i in range(ends)])  13.5 us
    ppermute x6, waiting for transfers between devices, extended(): lax.ppermute(tail, axis, [(i, (i + 1) % count) for i in range(ends)])  10.6 us
  transfers between devices with their start and end apart: 15, of which 10 were waited for; matrix products, arithmetic and copies ran while one was open for 3% of the time, Pallas kernels for 0%

commit v1 on v0

--- a/solution.py
+++ b/solution.py
@@ -102,7 +102,21 @@
     summed = lax.psum_scatter(jnp.stack([flow_x, flow_y]), "sec", scatter_dimension=0, tiled=True)
     rounded = summed[0].astype(jnp.bfloat16)
     row_blocks, per_row, block_size, _ = blocks.shape
-    piece = lax.all_gather(rounded, "gy", axis=2, tiled=True)
+    ways, here, step = (lax.axis_size("gy"), lax.axis_index("gy"), rounded.shape[2])
+    dims = [n * ways if d == 2 else n for d, n in enumerate(rounded.shape)]
+    full = lax.dynamic_update_slice_in_dim(
+        jnp.zeros(dims, rounded.dtype), rounded, here * step, axis=2
+    )
+    going_up = going_down = rounded
+    for far in range(1, ways // 2 + 1):
+        going_up = lax.ppermute(going_up, "gy", [(d, (d + 1) % ways) for d in range(ways)])
+        full = lax.dynamic_update_slice_in_dim(full, going_up, (here - far) % ways * step, axis=2)
+        if 2 * far < ways:
+            going_down = lax.ppermute(going_down, "gy", [(d, (d - 1) % ways) for d in range(ways)])
+            full = lax.dynamic_update_slice_in_dim(
+                full, going_down, (here + far) % ways * step, axis=2
+            )
+    piece = full
     count = piece.shape[2] // block_size
     split_rows = piece.reshape(layers, rows_x, count, block_size)
     block_ids = jnp.arange(count, dtype=jnp.int32)

time: 280 us -> 293 us (1.046)
  starting transfers between devices: 35.4 us -> 97.3 us
  waiting for transfers between devices: 206 us -> 157 us
    ppermute x0 -> x15, starting transfers between devices: none -> 62.1 us  [the longest x7 45.6 us: shards(): lax.ppermute(going_down, 'gy', [(d, (d - 1) % ways) for d in range(ways)])]
    all_gather x1 -> x0, waiting for transfers between devices: 52.4 us -> none  [shards(): piece = lax.all_gather(rounded, 'gy', axis=2, tiled=True)]
    ppermute x0 -> x15, waiting for transfers between devices: none -> 9.28 us  [the longest x8 9.26 us: shards(): lax.ppermute(going_up, 'gy', [(d, (d + 1) % ways) for d in range(ways)])]
    psum x1, waiting for transfers between devices: 70 us -> 65 us  [shards(): sensitivity = lax.psum(partial_sens, 'sec')]
  transfers between devices with their start and end apart: 15 -> 29, of which waited for: 10 -> 16; matrix products, arithmetic and copies ran while one was open for 3% -> 4% of each run, Pallas kernels for 0% -> 0%
where the time goes in v1:
time: 293 us; the launch traced here: 292 us
  waiting for transfers between devices  157 us (54%)
  starting transfers between devices  97.3 us (33%)
  between operations  15.1 us (5%)
  other arithmetic  12.6 us (4%)
  local copies, waits for them, and re-layouts  8.77 us (3%)
    psum x1, waiting for transfers between devices, shards(): sensitivity = lax.psum(partial_sens, 'sec')  65 us
    reduce_scatter x1, waiting for transfers between devices, shards(): lax.psum_scatter(jnp.stack([flow_x, flow_y]), 'sec', scatter_dimension=0,...  58.7 us
    ppermute x7, starting transfers between devices, shards(): lax.ppermute(going_down, 'gy', [(d, (d - 1) % ways) for d in range(ways)])  45.6 us
    ppermute x6, starting transfers between devices, extended(): lax.ppermute(tail, axis, [(i, (i + 1) % count) for i in range(ends)])  20.8 us
    ppermute x8, starting transfers between devices, shards(): lax.ppermute(going_up, 'gy', [(d, (d + 1) % ways) for d in range(ways)])  16.5 us
    ppermute x6, starting transfers between devices, extended(): lax.ppermute(head, axis, [((i + 1) % count, i) for i in range(ends)])  14.4 us
    ppermute x6, waiting for transfers between devices, extended(): lax.ppermute(head, axis, [((i + 1) % count, i) for i in range(ends)])  13.5 us
    ppermute x6, waiting for transfers between devices, extended(): lax.ppermute(tail, axis, [(i, (i + 1) % count) for i in range(ends)])  10.5 us
  transfers between devices with their start and end apart: 29, of which 16 were waited for; matrix products, arithmetic and copies ran while one was open for 4% of the time, Pallas kernels for 0%

profile of v1, /device:TPU:1, one launch (start us, length us, event | category | flops | bytes accessed | tf_op | source)
XLA Modules:
  0.0 291.7 jit_solution(5343175929800406602)
XLA Ops:
  8.3 4.9 %collective-permute-start.2 = (f32[16,1,256]{2,1,0:T(1,128)S(1)}, f32[16,1,256]{2,1,0:T(1,128)S(1)}, u32[]{:S(2)}, u32[]{:S(2)}) collective-permute-start(f32[16,1,256]{2,1,0:T(1,128)S(1)} %get-tuple-element.31), channel_id=1, source_target_pairs={{0,16},{16,32},{32,48},{48,64},{64,80},{80,96},{96,112},{112,128},... | collective-permute-start | bytes 49160 | tf_op jit(solution)/shard_map/ppermute | solution.py:15
  13.2 5.1 %collective-permute-start.3 = (f32[16,1,256]{2,1,0:T(1,128)S(1)}, f32[16,1,256]{2,1,0:T(1,128)S(1)}, u32[]{:S(2)}, u32[]{:S(2)}) collective-permute-start(f32[16,1,256]{2,1,0:T(1,128)S(1)} %get-tuple-element.32), channel_id=1, source_target_pairs={{16,0},{32,16},{48,32},{64,48},{80,64},{96,80},{112,96},{128,112},... | collective-permute-start | bytes 49160 | tf_op jit(solution)/shard_map/ppermute | solution.py:17
  19.5 1.9 collective-permute-start
  21.4 3.6 %collective-permute-start.1 = (f32[2,16,1,256]{3,2,1,0:T(1,128)S(1)}, f32[2,16,1,256]{3,2,1,0:T(1,128)S(1)}, u32[]{:S(2)}, u32[]{:S(2)}) collective-permute-start(f32[2,16,1,256]{3,2,1,0:T(1,128)S(1)} %get-tuple-element.22), channel_id=1, source_target_pairs={{0,16},{16,32},{32,48},{48,64},{64,80},{80,96},{96,112},{112,128},... | collective-permute-start | bytes 98312 | tf_op jit(solution)/shard_map/ppermute | solution.py:15
  35.0 4.1 %collective-permute-done.5 = f32[16,18,1]{2,1,0:T(8,128)S(1)} collective-permute-done((f32[16,18,1]{2,1,0:T(8,128)S(1)}, f32[16,18,1]{2,1,0:T(8,128)S(1)}, u32[]{:S(2)}, u32[]{:S(2)}) %collective-permute-start.5) | collective-permute-done | bytes 1184 | tf_op jit(solution)/shard_map/ppermute | solution.py:17
  39.9 2.2 collective-permute-start.6
  44.0 6.3 %collective-permute-done.6 = f32[2,16,18,1]{3,2,1,0:T(8,128)S(1)} collective-permute-done((f32[2,16,18,1]{3,2,1,0:T(8,128)S(1)}, f32[2,16,18,1]{3,2,1,0:T(8,128)S(1)}, u32[]{:S(2)}, u32[]{:S(2)}) %collective-permute-start.6) | collective-permute-done | bytes 2336 | tf_op jit(solution)/shard_map/ppermute | solution.py:15
  50.2 3.8 %collective-permute-done.7 = f32[2,16,18,1]{3,2,1,0:T(8,128)S(1)} collective-permute-done((f32[2,16,18,1]{3,2,1,0:T(8,128)S(1)}, f32[2,16,18,1]{3,2,1,0:T(8,128)S(1)}, u32[]{:S(2)}, u32[]{:S(2)}) %collective-permute-start.7) | collective-permute-done | bytes 2336 | tf_op jit(solution)/shard_map/ppermute | solution.py:17
  56.0 3.5 %collective-permute-start.8 = (f32[2,16,1,256]{3,2,1,0:T(1,128)S(1)}, f32[2,16,1,256]{3,2,1,0:T(1,128)S(1)}, u32[]{:S(2)}, u32[]{:S(2)}) collective-permute-start(f32[2,16,1,256]{3,2,1,0:T(1,128)S(1)} %get-tuple-element.17), channel_id=1, source_target_pairs={{16,0},{32,16},{48,32},{64,48},{80,64},{96,80},{112,96},{128,112},... | collective-permute-start | bytes 98312 | tf_op jit(solution)/shard_map/ppermute | solution.py:17
  59.4 3.7 %collective-permute-start.9 = (f32[2,16,1,256]{3,2,1,0:T(1,128)S(1)}, f32[2,16,1,256]{3,2,1,0:T(1,128)S(1)}, u32[]{:S(2)}, u32[]{:S(2)}) collective-permute-start(f32[2,16,1,256]{3,2,1,0:T(1,128)S(1)} %get-tuple-element.18), channel_id=1, source_target_pairs={{0,16},{16,32},{32,48},{48,64},{64,80},{80,96},{96,112},{112,128},... | collective-permute-start | bytes 98312 | tf_op jit(solution)/shard_map/ppermute | solution.py:15
  65.7 5.1 %collective-permute-start.11 = (f32[2,16,18,1]{3,2,1,0:T(8,128)S(1)}, f32[2,16,18,1]{3,2,1,0:T(8,128)S(1)}, u32[]{:S(2)}, u32[]{:S(2)}) collective-permute-start(f32[2,16,18,1]{3,2,1,0:T(8,128)S(1)} %get-tuple-element.14), channel_id=1, source_target_pairs={{0,1},{1,2},{2,3},{3,4},{4,5},{5,6},{6,7},{7,8},{8,9},{9,10},{10,1... | collective-permute-start | bytes 6920 | tf_op jit(solution)/shard_map/ppermute | solution.py:15
  71.4 5.6 %collective-permute-done.10 = f32[2,16,18,1]{3,2,1,0:T(8,128)S(1)} collective-permute-done((f32[2,16,18,1]{3,2,1,0:T(8,128)S(1)}, f32[2,16,18,1]{3,2,1,0:T(8,128)S(1)}, u32[]{:S(2)}, u32[]{:S(2)}) %collective-permute-start.10) | collective-permute-done | bytes 2336 | tf_op jit(solution)/shard_map/ppermute | solution.py:17
  77.0 1.8 collective-permute-done.11
  82.0 58.7 %reduce-scatter.2.cloned.1.call-done = f32[1,16,16,256]{3,2,1,0:T(8,128)} async-done(((f32[2,16,16,256]{3,2,1,0:T(8,128)}), f32[1,16,16,256]{3,2,1,0:T(8,128)}) %reduce-scatter.2.cloned.1.call-update) | async-done | bytes 262160 | tf_op jit(solution)/shard_map/reduce_scatter | solution.py:102
  141.7 3.1 %collective-permute-start.12 = (bf16[16,16,256]{2,1,0:T(8,128)(2,1)S(1)}, bf16[16,16,256]{2,1,0:T(8,128)(2,1)S(1)}, u32[]{:S(2)}, u32[]{:S(2)}) collective-permute-start(bf16[16,16,256]{2,1,0:T(8,128)(2,1)S(1)} %get-tuple-element.8), channel_id=1, source_target_pairs={{0,1},{1,2},{2,3},{3,4},{4,5},{5,6},{6,7},{7,8},{8,9},{9,10},{10,1... | collective-permute-start | bytes 393224 | tf_op jit(solution)/shard_map/ppermute | solution.py:112
  144.8 5.5 %collective-permute-start.13 = (bf16[16,16,256]{2,1,0:T(8,128)(2,1)S(1)}, bf16[16,16,256]{2,1,0:T(8,128)(2,1)S(1)}, u32[]{:S(2)}, u32[]{:S(2)}) collective-permute-start(bf16[16,16,256]{2,1,0:T(8,128)(2,1)S(1)} %get-tuple-element.8), channel_id=1, source_target_pairs={{0,15},{1,0},{2,1},{3,2},{4,3},{5,4},{6,5},{7,6},{8,7},{9,8},{10,9... | collective-permute-start | bytes 393224 | tf_op jit(solution)/shard_map/ppermute | solution.py:115
  151.4 1.9 collective-permute-start.14
  153.3 6.7 %collective-permute-start.15 = (bf16[16,16,256]{2,1,0:T(8,128)(2,1)S(1)}, bf16[16,16,256]{2,1,0:T(8,128)(2,1)S(1)}, u32[]{:S(2)}, u32[]{:S(2)}) collective-permute-start(bf16[16,16,256]{2,1,0:T(8,128)(2,1)S(1)} %collective-permute-done.13), channel_id=1, source_target_pairs={{0,15},{1,0},{2,1},{3,2},{4,3},{5,4},{6,5},{7,6},{8,7},{9,8},{10,9... | collective-permute-start | bytes 393224 | tf_op jit(solution)/shard_map/ppermute | solution.py:115
  160.4 1.9 collective-permute-start.16
  162.3 6.7 %collective-permute-start.17 = (bf16[16,16,256]{2,1,0:T(8,128)(2,1)S(1)}, bf16[16,16,256]{2,1,0:T(8,128)(2,1)S(1)}, u32[]{:S(2)}, u32[]{:S(2)}) collective-permute-start(bf16[16,16,256]{2,1,0:T(8,128)(2,1)S(1)} %collective-permute-done.15), channel_id=1, source_target_pairs={{0,15},{1,0},{2,1},{3,2},{4,3},{5,4},{6,5},{7,6},{8,7},{9,8},{10,9... | collective-permute-start | bytes 393224 | tf_op jit(solution)/shard_map/ppermute | solution.py:115
  169.4 1.9 collective-permute-start.18
  171.4 6.7 %collective-permute-start.19 = (bf16[16,16,256]{2,1,0:T(8,128)(2,1)S(1)}, bf16[16,16,256]{2,1,0:T(8,128)(2,1)S(1)}, u32[]{:S(2)}, u32[]{:S(2)}) collective-permute-start(bf16[16,16,256]{2,1,0:T(8,128)(2,1)S(1)} %collective-permute-done.17), channel_id=1, source_target_pairs={{0,15},{1,0},{2,1},{3,2},{4,3},{5,4},{6,5},{7,6},{8,7},{9,8},{10,9... | collective-permute-start | bytes 393224 | tf_op jit(solution)/shard_map/ppermute | solution.py:115
  178.4 1.9 collective-permute-start.20
  180.4 6.7 %collective-permute-start.21 = (bf16[16,16,256]{2,1,0:T(8,128)(2,1)S(1)}, bf16[16,16,256]{2,1,0:T(8,128)(2,1)S(1)}, u32[]{:S(2)}, u32[]{:S(2)}) collective-permute-start(bf16[16,16,256]{2,1,0:T(8,128)(2,1)S(1)} %collective-permute-done.19), channel_id=1, source_target_pairs={{0,15},{1,0},{2,1},{3,2},{4,3},{5,4},{6,5},{7,6},{8,7},{9,8},{10,9... | collective-permute-start | bytes 393224 | tf_op jit(solution)/shard_map/ppermute | solution.py:115
  187.5 1.9 collective-permute-start.22
  189.4 6.7 %collective-permute-start.23 = (bf16[16,16,256]{2,1,0:T(8,128)(2,1)S(1)}, bf16[16,16,256]{2,1,0:T(8,128)(2,1)S(1)}, u32[]{:S(2)}, u32[]{:S(2)}) collective-permute-start(bf16[16,16,256]{2,1,0:T(8,128)(2,1)S(1)} %collective-permute-done.21), channel_id=1, source_target_pairs={{0,15},{1,0},{2,1},{3,2},{4,3},{5,4},{6,5},{7,6},{8,7},{9,8},{10,9... | collective-permute-start | bytes 393224 | tf_op jit(solution)/shard_map/ppermute | solution.py:115
  196.5 1.9 collective-permute-start.24
  198.4 6.7 %collective-permute-start.25 = (bf16[16,16,256]{2,1,0:T(8,128)(2,1)S(1)}, bf16[16,16,256]{2,1,0:T(8,128)(2,1)S(1)}, u32[]{:S(2)}, u32[]{:S(2)}) collective-permute-start(bf16[16,16,256]{2,1,0:T(8,128)(2,1)S(1)} %collective-permute-done.23), channel_id=1, source_target_pairs={{0,15},{1,0},{2,1},{3,2},{4,3},{5,4},{6,5},{7,6},{8,7},{9,8},{10,9... | collective-permute-start | bytes 393224 | tf_op jit(solution)/shard_map/ppermute | solution.py:115
  205.5 1.9 collective-permute-start.26
  207.5 7.1 %collective-permute-done.26 = bf16[16,16,256]{2,1,0:T(8,128)(2,1)S(1)} collective-permute-done((bf16[16,16,256]{2,1,0:T(8,128)(2,1)S(1)}, bf16[16,16,256]{2,1,0:T(8,128)(2,1)S(1)}, u32[]{:S(2)}, u32[]{:S(2)}) %collective-permute-start.26) | collective-permute-done | bytes 131104 | tf_op jit(solution)/shard_map/ppermute | solution.py:112
  218.2 65.0 %all-reduce.5.cloned.1.call-done = f32[16,16,256]{2,1,0:T(8,128)} async-done(((f32[16,16,256]{2,1,0:T(8,128)}), f32[16,16,256]{2,1,0:T(8,128)}) %all-reduce.5.cloned.1.call-update) | async-done | bytes 262160 | tf_op jit(solution)/shard_map/psum | solution.py:130
  283.2 1.7 copy.42
  (120 shorter events, 30.5 us)
Async XLA Ops:
  7.2 208.6 %copy-start = (bf16[2,7,128,128]{3,2,1,0:T(8,128)(2,1)S(1)}, bf16[2,7,128,128]{3,2,1,0:T(8,128)(2,1)}, u32[]{:S(2)}) copy-start(bf16[2,7,128,128]{3,2,1,0:T(8,128)(2,1)} %param.18) | copy-start | bytes 1376260
  7.2 32.0 %copy-start.2 = (f32[16,16,256]{2,1,0:T(8,128)S(1)}, f32[16,16,256]{2,1,0:T(8,128)}, u32[]{:S(2)}) copy-start(f32[16,16,256]{2,1,0:T(8,128)} %param.12) | copy-start | bytes 786436
  7.2 133.6 %reduce-scatter.2.cloned.1.call-start = ((), (), s32[]{:S(2)}) async-start(), calls=%async_computation.1 | async-start | bytes 786432 | tf_op jit(solution)/shard_map/reduce_scatter | solution.py:102
  8.3 20.6 %collective-permute-start.2 = (f32[16,1,256]{2,1,0:T(1,128)S(1)}, f32[16,1,256]{2,1,0:T(1,128)S(1)}, u32[]{:S(2)}, u32[]{:S(2)}) collective-permute-start(f32[16,1,256]{2,1,0:T(1,128)S(1)} %get-tuple-element.31), channel_id=1, source_target_pairs={{0,16},{16,32},{32,48},{48,64},{64,80},{80,96},{96,112},{112,128},... | collective-permute-start | bytes 49160 | tf_op jit(solution)/shard_map/ppermute | solution.py:15
  13.2 15.7 %collective-permute-start.3 = (f32[16,1,256]{2,1,0:T(1,128)S(1)}, f32[16,1,256]{2,1,0:T(1,128)S(1)}, u32[]{:S(2)}, u32[]{:S(2)}) collective-permute-start(f32[16,1,256]{2,1,0:T(1,128)S(1)} %get-tuple-element.32), channel_id=1, source_target_pairs={{16,0},{32,16},{48,32},{64,48},{80,64},{96,80},{112,96},{128,112},... | collective-permute-start | bytes 49160 | tf_op jit(solution)/shard_map/ppermute | solution.py:17
  19.5 20.1 %collective-permute-start = (f32[2,16,1,256]{3,2,1,0:T(1,128)S(1)}, f32[2,16,1,256]{3,2,1,0:T(1,128)S(1)}, u32[]{:S(2)}, u32[]{:S(2)}) collective-permute-start(f32[2,16,1,256]{3,2,1,0:T(1,128)S(1)} %get-tuple-element.21), channel_id=1, source_target_pairs={{16,0},{32,16},{48,32},{64,48},{80,64},{96,80},{112,96},{128,112},... | collective-permute-start | bytes 98312 | tf_op jit(solution)/shard_map/ppermute | solution.py:17
  21.4 18.1 %collective-permute-start.1 = (f32[2,16,1,256]{3,2,1,0:T(1,128)S(1)}, f32[2,16,1,256]{3,2,1,0:T(1,128)S(1)}, u32[]{:S(2)}, u32[]{:S(2)}) collective-permute-start(f32[2,16,1,256]{3,2,1,0:T(1,128)S(1)} %get-tuple-element.22), channel_id=1, source_target_pairs={{0,16},{16,32},{32,48},{48,64},{64,80},{80,96},{96,112},{112,128},... | collective-permute-start | bytes 98312 | tf_op jit(solution)/shard_map/ppermute | solution.py:15
  30.1 5.0 %collective-permute-start.4 = (f32[16,18,1]{2,1,0:T(8,128)S(1)}, f32[16,18,1]{2,1,0:T(8,128)S(1)}, u32[]{:S(2)}, u32[]{:S(2)}) collective-permute-start(f32[16,18,1]{2,1,0:T(8,128)S(1)} %get-tuple-element.24), channel_id=1, source_target_pairs={{0,1},{1,2},{2,3},{3,4},{4,5},{5,6},{6,7},{7,8},{8,9},{9,10},{10,1... | collective-permute-start | bytes 3464 | tf_op jit(solution)/shard_map/ppermute | solution.py:15
  31.4 7.8 %collective-permute-start.5 = (f32[16,18,1]{2,1,0:T(8,128)S(1)}, f32[16,18,1]{2,1,0:T(8,128)S(1)}, u32[]{:S(2)}, u32[]{:S(2)}) collective-permute-start(f32[16,18,1]{2,1,0:T(8,128)S(1)} %get-tuple-element.23), channel_id=1, source_target_pairs={{1,0},{2,1},{3,2},{4,3},{5,4},{6,5},{7,6},{8,7},{9,8},{10,9},{11,1... | collective-permute-start | bytes 3464 | tf_op jit(solution)/shard_map/ppermute | solution.py:17
  39.9 10.4 %collective-permute-start.6 = (f32[2,16,18,1]{3,2,1,0:T(8,128)S(1)}, f32[2,16,18,1]{3,2,1,0:T(8,128)S(1)}, u32[]{:S(2)}, u32[]{:S(2)}) collective-permute-start(f32[2,16,18,1]{3,2,1,0:T(8,128)S(1)} %get-tuple-element.16), channel_id=1, source_target_pairs={{0,1},{1,2},{2,3},{3,4},{4,5},{5,6},{6,7},{7,8},{8,9},{9,10},{10,1... | collective-permute-start | bytes 6920 | tf_op jit(solution)/shard_map/ppermute | solution.py:15
  42.1 12.0 %collective-permute-start.7 = (f32[2,16,18,1]{3,2,1,0:T(8,128)S(1)}, f32[2,16,18,1]{3,2,1,0:T(8,128)S(1)}, u32[]{:S(2)}, u32[]{:S(2)}) collective-permute-start(f32[2,16,18,1]{3,2,1,0:T(8,128)S(1)} %get-tuple-element.15), channel_id=1, source_target_pairs={{1,0},{2,1},{3,2},{4,3},{5,4},{6,5},{7,6},{8,7},{9,8},{10,9},{11,1... | collective-permute-start | bytes 6920 | tf_op jit(solution)/shard_map/ppermute | solution.py:17
  55.9 14.9 %copy-start.13 = (bf16[2,2,16,16,256]{4,3,2,1,0:T(8,128)(2,1)S(1)}, bf16[2,2,16,16,256]{4,3,2,1,0:T(8,128)(2,1)}, u32[]{:S(2)}) copy-start(bf16[2,2,16,16,256]{4,3,2,1,0:T(8,128)(2,1)} %param.11) | copy-start | bytes 1572868
  56.0 7.1 %collective-permute-start.8 = (f32[2,16,1,256]{3,2,1,0:T(1,128)S(1)}, f32[2,16,1,256]{3,2,1,0:T(1,128)S(1)}, u32[]{:S(2)}, u32[]{:S(2)}) collective-permute-start(f32[2,16,1,256]{3,2,1,0:T(1,128)S(1)} %get-tuple-element.17), channel_id=1, source_target_pairs={{16,0},{32,16},{48,32},{64,48},{80,64},{96,80},{112,96},{128,112},... | collective-permute-start | bytes 98312 | tf_op jit(solution)/shard_map/ppermute | solution.py:17
  59.4 4.7 %collective-permute-start.9 = (f32[2,16,1,256]{3,2,1,0:T(1,128)S(1)}, f32[2,16,1,256]{3,2,1,0:T(1,128)S(1)}, u32[]{:S(2)}, u32[]{:S(2)}) collective-permute-start(f32[2,16,1,256]{3,2,1,0:T(1,128)S(1)} %get-tuple-element.18), channel_id=1, source_target_pairs={{0,16},{16,32},{32,48},{48,64},{64,80},{80,96},{96,112},{112,128},... | collective-permute-start | bytes 98312 | tf_op jit(solution)/shard_map/ppermute | solution.py:15
  64.4 12.6 %collective-permute-start.10 = (f32[2,16,18,1]{3,2,1,0:T(8,128)S(1)}, f32[2,16,18,1]{3,2,1,0:T(8,128)S(1)}, u32[]{:S(2)}, u32[]{:S(2)}) collective-permute-start(f32[2,16,18,1]{3,2,1,0:T(8,128)S(1)} %get-tuple-element.13), channel_id=1, source_target_pairs={{1,0},{2,1},{3,2},{4,3},{5,4},{6,5},{7,6},{8,7},{9,8},{10,9},{11,1... | collective-permute-start | bytes 6920 | tf_op jit(solution)/shard_map/ppermute | solution.py:17
  65.7 13.0 %collective-permute-start.11 = (f32[2,16,18,1]{3,2,1,0:T(8,128)S(1)}, f32[2,16,18,1]{3,2,1,0:T(8,128)S(1)}, u32[]{:S(2)}, u32[]{:S(2)}) collective-permute-start(f32[2,16,18,1]{3,2,1,0:T(8,128)S(1)} %get-tuple-element.14), channel_id=1, source_target_pairs={{0,1},{1,2},{2,3},{3,4},{4,5},{5,6},{6,7},{7,8},{8,9},{9,10},{10,1... | collective-permute-start | bytes 6920 | tf_op jit(solution)/shard_map/ppermute | solution.py:15
  81.0 202.3 %all-reduce.5.cloned.1.call-start = ((), (), s32[]{:S(2)}) async-start(), calls=%async_computation.2 | async-start | bytes 524288 | tf_op jit(solution)/shard_map/psum | solution.py:130
  141.7 9.7 %collective-permute-start.12 = (bf16[16,16,256]{2,1,0:T(8,128)(2,1)S(1)}, bf16[16,16,256]{2,1,0:T(8,128)(2,1)S(1)}, u32[]{:S(2)}, u32[]{:S(2)}) collective-permute-start(bf16[16,16,256]{2,1,0:T(8,128)(2,1)S(1)} %get-tuple-element.8), channel_id=1, source_target_pairs={{0,1},{1,2},{2,3},{3,4},{4,5},{5,6},{6,7},{7,8},{8,9},{9,10},{10,1... | collective-permute-start | bytes 393224 | tf_op jit(solution)/shard_map/ppermute | solution.py:112
  144.8 8.5 %collective-permute-start.13 = (bf16[16,16,256]{2,1,0:T(8,128)(2,1)S(1)}, bf16[16,16,256]{2,1,0:T(8,128)(2,1)S(1)}, u32[]{:S(2)}, u32[]{:S(2)}) collective-permute-start(bf16[16,16,256]{2,1,0:T(8,128)(2,1)S(1)} %get-tuple-element.8), channel_id=1, source_target_pairs={{0,15},{1,0},{2,1},{3,2},{4,3},{5,4},{6,5},{7,6},{8,7},{9,8},{10,9... | collective-permute-start | bytes 393224 | tf_op jit(solution)/shard_map/ppermute | solution.py:115
  151.4 9.0 %collective-permute-start.14 = (bf16[16,16,256]{2,1,0:T(8,128)(2,1)S(1)}, bf16[16,16,256]{2,1,0:T(8,128)(2,1)S(1)}, u32[]{:S(2)}, u32[]{:S(2)}) collective-permute-start(bf16[16,16,256]{2,1,0:T(8,128)(2,1)S(1)} %collective-permute-done.12), channel_id=1, source_target_pairs={{0,1},{1,2},{2,3},{3,4},{4,5},{5,6},{6,7},{7,8},{8,9},{9,10},{10,1... | collective-permute-start | bytes 393224 | tf_op jit(solution)/shard_map/ppermute | solution.py:112
  153.3 9.0 %collective-permute-start.15 = (bf16[16,16,256]{2,1,0:T(8,128)(2,1)S(1)}, bf16[16,16,256]{2,1,0:T(8,128)(2,1)S(1)}, u32[]{:S(2)}, u32[]{:S(2)}) collective-permute-start(bf16[16,16,256]{2,1,0:T(8,128)(2,1)S(1)} %collective-permute-done.13), channel_id=1, source_target_pairs={{0,15},{1,0},{2,1},{3,2},{4,3},{5,4},{6,5},{7,6},{8,7},{9,8},{10,9... | collective-permute-start | bytes 393224 | tf_op jit(solution)/shard_map/ppermute | solution.py:115
  160.4 9.0 %collective-permute-start.16 = (bf16[16,16,256]{2,1,0:T(8,128)(2,1)S(1)}, bf16[16,16,256]{2,1,0:T(8,128)(2,1)S(1)}, u32[]{:S(2)}, u32[]{:S(2)}) collective-permute-start(bf16[16,16,256]{2,1,0:T(8,128)(2,1)S(1)} %collective-permute-done.14), channel_id=1, source_target_pairs={{0,1},{1,2},{2,3},{3,4},{4,5},{5,6},{6,7},{7,8},{8,9},{9,10},{10,1... | collective-permute-start | bytes 393224 | tf_op jit(solution)/shard_map/ppermute | solution.py:112
  162.3 9.0 %collective-permute-start.17 = (bf16[16,16,256]{2,1,0:T(8,128)(2,1)S(1)}, bf16[16,16,256]{2,1,0:T(8,128)(2,1)S(1)}, u32[]{:S(2)}, u32[]{:S(2)}) collective-permute-start(bf16[16,16,256]{2,1,0:T(8,128)(2,1)S(1)} %collective-permute-done.15), channel_id=1, source_target_pairs={{0,15},{1,0},{2,1},{3,2},{4,3},{5,4},{6,5},{7,6},{8,7},{9,8},{10,9... | collective-permute-start | bytes 393224 | tf_op jit(solution)/shard_map/ppermute | solution.py:115
  169.4 9.0 %collective-permute-start.18 = (bf16[16,16,256]{2,1,0:T(8,128)(2,1)S(1)}, bf16[16,16,256]{2,1,0:T(8,128)(2,1)S(1)}, u32[]{:S(2)}, u32[]{:S(2)}) collective-permute-start(bf16[16,16,256]{2,1,0:T(8,128)(2,1)S(1)} %collective-permute-done.16), channel_id=1, source_target_pairs={{0,1},{1,2},{2,3},{3,4},{4,5},{5,6},{6,7},{7,8},{8,9},{9,10},{10,1... | collective-permute-start | bytes 393224 | tf_op jit(solution)/shard_map/ppermute | solution.py:112
  171.4 9.0 %collective-permute-start.19 = (bf16[16,16,256]{2,1,0:T(8,128)(2,1)S(1)}, bf16[16,16,256]{2,1,0:T(8,128)(2,1)S(1)}, u32[]{:S(2)}, u32[]{:S(2)}) collective-permute-start(bf16[16,16,256]{2,1,0:T(8,128)(2,1)S(1)} %collective-permute-done.17), channel_id=1, source_target_pairs={{0,15},{1,0},{2,1},{3,2},{4,3},{5,4},{6,5},{7,6},{8,7},{9,8},{10,9... | collective-permute-start | bytes 393224 | tf_op jit(solution)/shard_map/ppermute | solution.py:115
  178.4 9.0 %collective-permute-start.20 = (bf16[16,16,256]{2,1,0:T(8,128)(2,1)S(1)}, bf16[16,16,256]{2,1,0:T(8,128)(2,1)S(1)}, u32[]{:S(2)}, u32[]{:S(2)}) collective-permute-start(bf16[16,16,256]{2,1,0:T(8,128)(2,1)S(1)} %collective-permute-done.18), channel_id=1, source_target_pairs={{0,1},{1,2},{2,3},{3,4},{4,5},{5,6},{6,7},{7,8},{8,9},{9,10},{10,1... | collective-permute-start | bytes 393224 | tf_op jit(solution)/shard_map/ppermute | solution.py:112
  180.4 9.0 %collective-permute-start.21 = (bf16[16,16,256]{2,1,0:T(8,128)(2,1)S(1)}, bf16[16,16,256]{2,1,0:T(8,128)(2,1)S(1)}, u32[]{:S(2)}, u32[]{:S(2)}) collective-permute-start(bf16[16,16,256]{2,1,0:T(8,128)(2,1)S(1)} %collective-permute-done.19), channel_id=1, source_target_pairs={{0,15},{1,0},{2,1},{3,2},{4,3},{5,4},{6,5},{7,6},{8,7},{9,8},{10,9... | collective-permute-start | bytes 393224 | tf_op jit(solution)/shard_map/ppermute | solution.py:115
  187.5 9.0 %collective-permute-start.22 = (bf16[16,16,256]{2,1,0:T(8,128)(2,1)S(1)}, bf16[16,16,256]{2,1,0:T(8,128)(2,1)S(1)}, u32[]{:S(2)}, u32[]{:S(2)}) collective-permute-start(bf16[16,16,256]{2,1,0:T(8,128)(2,1)S(1)} %collective-permute-done.20), channel_id=1, source_target_pairs={{0,1},{1,2},{2,3},{3,4},{4,5},{5,6},{6,7},{7,8},{8,9},{9,10},{10,1... | collective-permute-start | bytes 393224 | tf_op jit(solution)/shard_map/ppermute | solution.py:112
  189.4 9.0 %collective-permute-start.23 = (bf16[16,16,256]{2,1,0:T(8,128)(2,1)S(1)}, bf16[16,16,256]{2,1,0:T(8,128)(2,1)S(1)}, u32[]{:S(2)}, u32[]{:S(2)}) collective-permute-start(bf16[16,16,256]{2,1,0:T(8,128)(2,1)S(1)} %collective-permute-done.21), channel_id=1, source_target_pairs={{0,15},{1,0},{2,1},{3,2},{4,3},{5,4},{6,5},{7,6},{8,7},{9,8},{10,9... | collective-permute-start | bytes 393224 | tf_op jit(solution)/shard_map/ppermute | solution.py:115
  196.5 9.0 %collective-permute-start.24 = (bf16[16,16,256]{2,1,0:T(8,128)(2,1)S(1)}, bf16[16,16,256]{2,1,0:T(8,128)(2,1)S(1)}, u32[]{:S(2)}, u32[]{:S(2)}) collective-permute-start(bf16[16,16,256]{2,1,0:T(8,128)(2,1)S(1)} %collective-permute-done.22), channel_id=1, source_target_pairs={{0,1},{1,2},{2,3},{3,4},{4,5},{5,6},{6,7},{7,8},{8,9},{9,10},{10,1... | collective-permute-start | bytes 393224 | tf_op jit(solution)/shard_map/ppermute | solution.py:112
  198.4 9.0 %collective-permute-start.25 = (bf16[16,16,256]{2,1,0:T(8,128)(2,1)S(1)}, bf16[16,16,256]{2,1,0:T(8,128)(2,1)S(1)}, u32[]{:S(2)}, u32[]{:S(2)}) collective-permute-start(bf16[16,16,256]{2,1,0:T(8,128)(2,1)S(1)} %collective-permute-done.23), channel_id=1, source_target_pairs={{0,15},{1,0},{2,1},{3,2},{4,3},{5,4},{6,5},{7,6},{8,7},{9,8},{10,9... | collective-permute-start | bytes 393224 | tf_op jit(solution)/shard_map/ppermute | solution.py:115
  205.5 9.1 %collective-permute-start.26 = (bf16[16,16,256]{2,1,0:T(8,128)(2,1)S(1)}, bf16[16,16,256]{2,1,0:T(8,128)(2,1)S(1)}, u32[]{:S(2)}, u32[]{:S(2)}) collective-permute-start(bf16[16,16,256]{2,1,0:T(8,128)(2,1)S(1)} %collective-permute-done.24), channel_id=1, source_target_pairs={{0,1},{1,2},{2,3},{3,4},{4,5},{5,6},{6,7},{7,8},{8,9},{9,10},{10,1... | collective-permute-start | bytes 393224 | tf_op jit(solution)/shard_map/ppermute | solution.py:112
  (16 other events, 133.5 us)
Sparse Core Ops, SparseCore 0:
  81.1 59.6 reduce-scatter.1
  217.2 65.9 all-reduce.4
